TPU v7x, 32 devices: a whole 2x2x4 slice. The times are simulated.
32 devices in a mesh: dp: 4 (over y, x), feat: 8 (over z, core).
Axes of the slice: x: 2, y: 2, z: 4, core: 2. Of those that a mesh axis runs over, the one named last changes fastest.
Arguments:
- sketches: bfloat16 [4, 256, 65536], P('dp', None, 'feat'), may hold values from -24 to 24
Outputs:
- merged: bfloat16 [4, 256, 65536], P('dp', None, 'feat')
All inputs are finite; a program needn't handle non-finite values.
Results may differ from a plain program's by a relative error of at most 0.001.
The roundings to bfloat16 on the way count: a program that leaves them out, or rounds other values in their place, can miss the bound.
Values may be sent and summed in bfloat16 or wider, within the bound.
No kernel may reach another device: no remote copies, remote signals or barrier semaphores. Data moves between devices by JAX's collectives and lax.ppermute only.
A program may use at most 128 MiB of HBM per device.

v0:
```python
import jax
import jax.numpy as jnp
from jax import lax
from jax.sharding import PartitionSpec as P

LEVELS = 2


def from_partner(block, axis, stride):
    count = lax.axis_size(axis)
    route = []
    for low in range(count):
        high = low | 1 << stride
        if high != low and high < count:
            route += [(low, high), (high, low)]
    return lax.ppermute(block, axis, route)


def solve_rows(gram, count):
    size = gram.shape[0]
    average = jnp.trace(gram) / size
    kernel = jnp.eye(size, dtype=jnp.float32) + gram / average
    factor = jnp.linalg.cholesky(kernel)
    target = jnp.eye(size, count, dtype=jnp.float32)
    middle = lax.linalg.triangular_solve(factor, target, left_side=True, lower=True)
    inverse = lax.linalg.triangular_solve(
        factor, middle, left_side=True, lower=True, transpose_a=True
    )
    return inverse.T.astype(jnp.bfloat16)


def per_device(sketches):
    current = sketches[0]
    count = current.shape[0]
    position = lax.axis_index("dp")
    for level in range(LEVELS):
        is_lower = position // 2**level % 2 == 0
        partner = from_partner(current, "dp", level)
        lower = jnp.where(is_lower, current, partner)
        upper = jnp.where(is_lower, partner, current)
        stacked = jnp.concatenate([lower, upper], axis=0)
        partial_gram = jnp.dot(stacked, stacked.T, preferred_element_type=jnp.float32)
        gram_total = lax.psum(partial_gram, "feat")
        weights = solve_rows(gram_total, count)
        update = jnp.dot(weights, stacked, preferred_element_type=jnp.float32)
        fresh = (lower.astype(jnp.float32) - update).astype(jnp.bfloat16)
        current = fresh
    return current[None]


def solution(mesh):
    placed = (P("dp", None, "feat"),)
    return jax.shard_map(
        per_device, mesh=mesh, in_specs=placed, out_specs=P("dp", None, "feat"), check_vma=False
    )
```

profile of v0, /device:TPU:0, one launch (start us, length us, event | category | flops | bytes accessed | tf_op | source)
XLA Modules:
  0.0 661.4 jit_solution(7594506524148744572)
XLA Ops:
  9.5 90.9 %collective-permute-done = bf16[256,8192]{1,0:T(8,128)(2,1)} collective-permute-done((bf16[256,8192]{1,0:T(8,128)(2,1)}, bf16[256,8192]{1,0:T(8,128)(2,1)}, u32[]{:S(2)}, u32[]{:S(2)}) %collective-permute-start) | collective-permute-done | bytes 4194336 | tf_op jit(solution)/shard_map/ppermute | solution.py:16
  107.4 9.1 %fusion.4 = f32[512,512]{0,1:T(8,128)} fusion(bf16[256,8192]{1,0:T(8,128)(2,1)S(1)} %get-tuple-element.62, bf16[256,8192]{1,0:T(8,128)(2,1)} %get-tuple-element.63), kind=kOutput, calls=%fused_computation.12 | convolution fusion | flops 4311744512 | bytes 9437184 | tf_op jit(solution)/shard_map/dot_general | solution.py:42
  117.1 60.3 %all-reduce.4.cloned.1.call-done = f32[512,512]{0,1:T(8,128)} async-done(((f32[512,512]{0,1:T(8,128)}), f32[512,512]{0,1:T(8,128)}) %all-reduce.4.cloned.1.call-update) | async-done | bytes 1048592 | tf_op jit(solution)/shard_map/psum | solution.py:43
  185.2 11.7 %cholesky.286 = f32[128,128]{1,0:T(8,128)S(1)} custom-call(f32[128,128]{1,0:T(8,128)S(1)} %cholesky.426), custom_call_target="Cholesky" | custom-call | tf_op jit(solution)/shard_map/jit(cholesky)/cholesky | solution.py:23
  197.1 9.8 %custom-call.31 = f32[1,128,128]{1,2,0:T(8,128)S(1)} custom-call(f32[1,128,128]{2,1,0:T(8,128)S(1)} %get-tuple-element.83), custom_call_target="InvertDiagBlocksLowerTriangular" | custom-call | tf_op jit(solution)/shard_map/jit(cholesky)/cholesky | solution.py:23
  209.4 11.7 %cholesky.305 = f32[128,128]{1,0:T(8,128)S(1)} custom-call(f32[128,128]{1,0:T(8,128)S(1)} %cholesky.430), custom_call_target="Cholesky" | custom-call | tf_op jit(solution)/shard_map/jit(cholesky)/cholesky | solution.py:23
  221.2 10.0 %custom-call.32 = f32[1,128,128]{1,2,0:T(8,128)S(1)} custom-call(f32[1,128,128]{2,1,0:T(8,128)S(1)} %get-tuple-element.80), custom_call_target="InvertDiagBlocksLowerTriangular" | custom-call | tf_op jit(solution)/shard_map/jit(cholesky)/cholesky | solution.py:23
  232.7 11.7 %cholesky.326 = f32[128,128]{1,0:T(8,128)S(1)} custom-call(f32[128,128]{1,0:T(8,128)S(1)} %cholesky.435), custom_call_target="Cholesky" | custom-call | tf_op jit(solution)/shard_map/jit(cholesky)/cholesky | solution.py:23
  245.1 9.8 %custom-call.33 = f32[1,128,128]{1,2,0:T(8,128)S(1)} custom-call(f32[1,128,128]{2,1,0:T(8,128)S(1)} %get-tuple-element.77), custom_call_target="InvertDiagBlocksLowerTriangular" | custom-call | tf_op jit(solution)/shard_map/jit(cholesky)/cholesky | solution.py:23
  256.4 11.9 %cholesky.343 = f32[128,128]{1,0:T(8,128)S(1)} custom-call(f32[128,128]{1,0:T(8,128)S(1)} %convolution_subtract_fusion.17), custom_call_target="Cholesky" | custom-call | tf_op jit(solution)/shard_map/jit(cholesky)/cholesky | solution.py:23
  280.6 39.3 %custom-call.35 = f32[4,128,128]{1,2,0:T(8,128)S(1)} custom-call(f32[4,128,128]{2,1,0:T(8,128)S(1)} %get-tuple-element.37), custom_call_target="InvertDiagBlocksLowerTriangular" | custom-call | tf_op jit(solution)/shard_map/triangular_solve/custom-call.8 | solution.py:26
  324.4 8.1 %subtract_convert_fusion.1 = bf16[256,8192]{1,0:T(8,128)(2,1)} fusion(bf16[256,8192]{1,0:T(8,128)(2,1)} %get-tuple-element.63, bf16[256,8192]{1,0:T(8,128)(2,1)S(1)} %copy-done.3, f32[128,256]{1,0:T(8,128)S(1)} %fusion.84, f32[128,256]{1,0:T(8,128)S(1)} %fusion.82, f32[128,256]{1,0:T(8,128)S(1)} %fusion.80, bf16[128,256]{1,0:T(8,128)(2,1)S(1)} %fusion.78), kind=kOutput, calls=%fused_computation.7 | convolution fusion | flops 2171600896 | bytes 13041664 | tf_op jit(solution)/shard_map/dot_general | solution.py:45
  334.0 89.4 %collective-permute-done.1 = bf16[256,8192]{1,0:T(8,128)(2,1)} collective-permute-done((bf16[256,8192]{1,0:T(8,128)(2,1)}, bf16[256,8192]{1,0:T(8,128)(2,1)}, u32[]{:S(2)}, u32[]{:S(2)}) %collective-permute-start.1) | collective-permute-done | bytes 4194336 | tf_op jit(solution)/shard_map/ppermute | solution.py:16
  430.9 9.0 %fusion.1 = f32[512,512]{0,1:T(8,128)} fusion(bf16[256,8192]{1,0:T(8,128)(2,1)} %get-tuple-element.61, bf16[256,8192]{1,0:T(8,128)(2,1)S(1)} %get-tuple-element.60), kind=kOutput, calls=%fused_computation.9 | convolution fusion | flops 4311744512 | bytes 9437184 | tf_op jit(solution)/shard_map/dot_general | solution.py:42
  440.0 59.3 %all-reduce.6.cloned.1.call-done = f32[512,512]{0,1:T(8,128)} async-done(((f32[512,512]{0,1:T(8,128)}), f32[512,512]{0,1:T(8,128)}) %all-reduce.6.cloned.1.call-update) | async-done | bytes 1048592 | tf_op jit(solution)/shard_map/psum | solution.py:43
  507.2 11.7 %cholesky.358 = f32[128,128]{1,0:T(8,128)S(1)} custom-call(f32[128,128]{1,0:T(8,128)S(1)} %cholesky.439), custom_call_target="Cholesky" | custom-call | tf_op jit(solution)/shard_map/jit(cholesky)/cholesky | solution.py:23
  519.1 9.8 %custom-call.36 = f32[1,128,128]{1,2,0:T(8,128)S(1)} custom-call(f32[1,128,128]{2,1,0:T(8,128)S(1)} %get-tuple-element.73), custom_call_target="InvertDiagBlocksLowerTriangular" | custom-call | tf_op jit(solution)/shard_map/jit(cholesky)/cholesky | solution.py:23
  531.4 11.9 %cholesky.377 = f32[128,128]{1,0:T(8,128)S(1)} custom-call(f32[128,128]{1,0:T(8,128)S(1)} %cholesky.443), custom_call_target="Cholesky" | custom-call | tf_op jit(solution)/shard_map/jit(cholesky)/cholesky | solution.py:23
  544.7 9.8 %custom-call.37 = f32[1,128,128]{1,2,0:T(8,128)S(1)} custom-call(f32[1,128,128]{2,1,0:T(8,128)S(1)} %get-tuple-element.70), custom_call_target="InvertDiagBlocksLowerTriangular" | custom-call | tf_op jit(solution)/shard_map/jit(cholesky)/cholesky | solution.py:23
  556.0 11.7 %cholesky.398 = f32[128,128]{1,0:T(8,128)S(1)} custom-call(f32[128,128]{1,0:T(8,128)S(1)} %cholesky.448), custom_call_target="Cholesky" | custom-call | tf_op jit(solution)/shard_map/jit(cholesky)/cholesky | solution.py:23
  568.5 9.8 %custom-call.38 = f32[1,128,128]{1,2,0:T(8,128)S(1)} custom-call(f32[1,128,128]{2,1,0:T(8,128)S(1)} %get-tuple-element.67), custom_call_target="InvertDiagBlocksLowerTriangular" | custom-call | tf_op jit(solution)/shard_map/jit(cholesky)/cholesky | solution.py:23
  579.9 11.7 %cholesky.415 = f32[128,128]{1,0:T(8,128)S(1)} custom-call(f32[128,128]{1,0:T(8,128)S(1)} %convolution_subtract_fusion.16), custom_call_target="Cholesky" | custom-call | tf_op jit(solution)/shard_map/jit(cholesky)/cholesky | solution.py:23
  595.1 8.1 %while.9 = (s32[]{:T(128)}, f32[512,512]{1,0:T(8,128)S(1)}, s32[4,2]{0,1:T(2,128)S(1)}, f32[4,128,128]{2,1,0:T(8,128)S(1)}, s32[]{:T(128)}) while((s32[]{:T(128)}, f32[512,512]{1,0:T(8,128)S(1)}, s32[4,2]{0,1:T(2,128)S(1)}, f32[4,128,128]{2,1,0:T(8,128)S(1)}, s32[]{:T(128)}) %tuple.71), condition=%wide.while_cond.1.clone, body=%wide.while_body.1.clone.sunk | while | flops 2 | bytes 131181 | solution.py:26
  603.3 39.6 %custom-call.40 = f32[4,128,128]{1,2,0:T(8,128)S(1)} custom-call(f32[4,128,128]{2,1,0:T(8,128)S(1)} %get-tuple-element.39), custom_call_target="InvertDiagBlocksLowerTriangular" | custom-call | tf_op jit(solution)/shard_map/triangular_solve/custom-call.8 | solution.py:26
  (128 shorter events, 90.6 us)
Async XLA Ops:
  6.5 170.9 %all-reduce.4.cloned.1.call-start = ((), (), s32[]{:S(2)}) async-start(), calls=%async_computation | async-start | bytes 2097152 | tf_op jit(solution)/shard_map/psum | solution.py:43
  6.5 93.9 %collective-permute-start = (bf16[256,8192]{1,0:T(8,128)(2,1)}, bf16[256,8192]{1,0:T(8,128)(2,1)}, u32[]{:S(2)}, u32[]{:S(2)}) collective-permute-start(bf16[256,8192]{1,0:T(8,128)(2,1)} %bitcast.133), channel_id=1, source_target_pairs={{0,8},{8,0},{16,24},{24,16},{1,9},{9,1},{17,25},{25,17},{2,10},{10... | collective-permute-start | bytes 12582920 | tf_op jit(solution)/shard_map/ppermute | solution.py:16
  105.5 1.9 copy-start.2
  116.5 382.7 %all-reduce.6.cloned.1.call-start = ((), (), s32[]{:S(2)}) async-start(), calls=%async_computation.1 | async-start | bytes 2097152 | tf_op jit(solution)/shard_map/psum | solution.py:43
  177.4 5.4 copy-start
  184.2 1.0 copy-start.7
  319.9 4.5 copy-start.3
  332.6 90.8 %collective-permute-start.1 = (bf16[256,8192]{1,0:T(8,128)(2,1)}, bf16[256,8192]{1,0:T(8,128)(2,1)}, u32[]{:S(2)}, u32[]{:S(2)}) collective-permute-start(bf16[256,8192]{1,0:T(8,128)(2,1)} %subtract_convert_fusion.1), channel_id=1, source_target_pairs={{0,16},{16,0},{8,24},{24,8},{1,17},{17,1},{9,25},{25,9},{2,18},{18... | collective-permute-start | bytes 12582920 | tf_op jit(solution)/shard_map/ppermute | solution.py:16
  428.9 2.0 copy-start.4
  499.2 5.5 copy-start.1
  506.2 1.0 copy-start.6
  642.9 4.5 copy-start.5
Sparse Core Ops, SparseCore 0:
  116.6 60.7 all-reduce.3
  440.1 59.1 all-reduce.5
where the time goes:
time: 666 us; the launch traced here: 661 us
  waiting for transfers between devices  300 us (45%)
  other arithmetic  258 us (39%)
  matrix products  53 us (8%)
  local copies, waits for them, and re-layouts  25.1 us (4%)
  between operations  20.7 us (3%)
    ppermute x2, waiting for transfers between devices, from_partner(): return lax.ppermute(block, axis, route)  180 us
    another operation x29, other arithmetic, solve_rows(): factor = jnp.linalg.cholesky(kernel)  158 us
    psum x2, waiting for transfers between devices, per_device(): gram_total = lax.psum(partial_gram, 'feat')  120 us
    another operation x5, other arithmetic, solve_rows(): lax.linalg.triangular_solve(factor, middle, left_side=True, lower=True, t...  79.1 us
    dot_general x2, matrix products, per_device(): jnp.dot(stacked, stacked.T, preferred_element_type=jnp.float32)  18.1 us
    another operation x27, local copies, waits for them, and re-layouts, solve_rows(): lax.linalg.triangular_solve(factor, middle, left_side=True, lower=True, t...  16.1 us
    dot_general x2, matrix products, per_device(): update = jnp.dot(weights, stacked, preferred_element_type=jnp.float32)  15 us
  transfers between devices with their start and end apart: 4, of which 4 were waited for; matrix products, arithmetic and copies ran while one was open for 0% of the time, Pallas kernels for 0%

commit v1 on v0

--- a/solution.py
+++ b/solution.py
@@ -1,9 +1,29 @@
+import functools
 import jax
 import jax.numpy as jnp
 from jax import lax
 from jax.sharding import PartitionSpec as P
+from jax.lax import axis_size, ppermute
 
 LEVELS = 2
+
+
+def check_threads(vals, row_axis):
+    axis_n = axis_size(row_axis)
+
+    def write_patch_for(known, s_next):
+        if s_next >= axis_n:
+            return known
+        return write_patch_for(
+            known
+            + ppermute(known, axis_name=row_axis, perm=[(i0, i0 ^ s_next) for i0 in range(axis_n)]),
+            2 * s_next,
+        )
+
+    return write_patch_for(vals, 1)
+
+
+scan_yards_up = functools.partial(check_threads, row_axis="feat")
 
 
 def from_partner(block, axis, stride):
@@ -40,7 +60,7 @@
         upper = jnp.where(is_lower, partner, current)
         stacked = jnp.concatenate([lower, upper], axis=0)
         partial_gram = jnp.dot(stacked, stacked.T, preferred_element_type=jnp.float32)
-        gram_total = lax.psum(partial_gram, "feat")
+        gram_total = scan_yards_up(partial_gram)
         weights = solve_rows(gram_total, count)
         update = jnp.dot(weights, stacked, preferred_element_type=jnp.float32)
         fresh = (lower.astype(jnp.float32) - update).astype(jnp.bfloat16)

time: 666 us -> 699 us (1.050)
  waiting for transfers between devices: 300 us -> 324 us
  between operations: 20.7 us -> 7.5 us
  starting transfers between devices: 4.95 us -> 14.5 us
  other arithmetic: 258 us -> 267 us
    ppermute x0 -> x6, waiting for transfers between devices: none -> 143 us  [write_patch_for(): ppermute(known, axis_name=row_axis, perm=[(i0, i0 ^ s_next) for i0 in ran...]
    psum x2 -> x0, waiting for transfers between devices: 120 us -> none  [per_device(): gram_total = lax.psum(partial_gram, 'feat')]
    ppermute x0 -> x6, starting transfers between devices: none -> 9.99 us  [write_patch_for(): ppermute(known, axis_name=row_axis, perm=[(i0, i0 ^ s_next) for i0 in ran...]
    another operation x29, other arithmetic: 158 us -> 168 us  [solve_rows(): factor = jnp.linalg.cholesky(kernel)]
  transfers between devices with their start and end apart: 4 -> 8, of which waited for: 4 -> 8; matrix products, arithmetic and copies ran while one was open for 0% -> 0% of each run, Pallas kernels for 0% -> 0%
where the time goes in v1:
time: 699 us; the launch traced here: 690 us
  waiting for transfers between devices  324 us (46%)
  other arithmetic  267 us (38%)
  matrix products  55.9 us (8%)
  local copies, waits for them, and re-layouts  20.7 us (3%)
  starting transfers between devices  14.5 us (2%)
  between operations  7.5 us (1%)
    ppermute x2, waiting for transfers between devices, from_partner(): return lax.ppermute(block, axis, route)  181 us
    another operation x29, other arithmetic, solve_rows(): factor = jnp.linalg.cholesky(kernel)  168 us
    ppermute x6, waiting for transfers between devices, write_patch_for(): ppermute(known, axis_name=row_axis, perm=[(i0, i0 ^ s_next) for i0 in ran...  143 us
    another operation x5, other arithmetic, solve_rows(): lax.linalg.triangular_solve(factor, middle, left_side=True, lower=True, t...  79.1 us
    dot_general x2, matrix products, per_device(): jnp.dot(stacked, stacked.T, preferred_element_type=jnp.float32)  21 us
    another operation x27, local copies, waits for them, and re-layouts, solve_rows(): lax.linalg.triangular_solve(factor, middle, left_side=True, lower=True, t...  15.8 us
    dot_general x2, matrix products, per_device(): update = jnp.dot(weights, stacked, preferred_element_type=jnp.float32)  15 us
  transfers between devices with their start and end apart: 8, of which 8 were waited for; matrix products, arithmetic and copies ran while one was open for 0% of the time, Pallas kernels for 0%

profile of v1, /device:TPU:0, one launch (start us, length us, event | category | flops | bytes accessed | tf_op | source)
XLA Modules:
  0.0 689.7 jit_solution(15332466483529554168)
XLA Ops:
  3.0 90.9 %collective-permute-done = bf16[256,8192]{1,0:T(8,128)(2,1)} collective-permute-done((bf16[256,8192]{1,0:T(8,128)(2,1)}, bf16[256,8192]{1,0:T(8,128)(2,1)}, u32[]{:S(2)}, u32[]{:S(2)}) %collective-permute-start) | collective-permute-done | bytes 4194336 | tf_op jit(solution)/shard_map/ppermute | solution.py:36
  98.9 10.5 %fusion.4 = f32[512,512]{0,1:T(8,128)} fusion(bf16[256,8192]{1,0:T(8,128)(2,1)S(1)} %get-tuple-element.66, bf16[256,8192]{1,0:T(8,128)(2,1)} %get-tuple-element.67), kind=kOutput, calls=%fused_computation.12 | convolution fusion | flops 4311744512 | bytes 9437184 | tf_op jit(solution)/shard_map/dot_general | solution.py:62
  115.7 23.5 %collective-permute-done.2 = f32[512,512]{0,1:T(8,128)S(1)} collective-permute-done((f32[512,512]{0,1:T(8,128)S(1)}, f32[512,512]{0,1:T(8,128)S(1)}, u32[]{:S(2)}, u32[]{:S(2)}) %collective-permute-start.2) | collective-permute-done | bytes 1048608 | tf_op jit(solution)/shard_map/ppermute | solution.py:19
  142.2 45.1 %collective-permute-done.3 = f32[512,512]{0,1:T(8,128)} collective-permute-done((f32[512,512]{0,1:T(8,128)S(1)}, f32[512,512]{0,1:T(8,128)}, u32[]{:S(2)}, u32[]{:S(2)}) %collective-permute-start.3) | collective-permute-done | bytes 1048608 | tf_op jit(solution)/shard_map/ppermute | solution.py:19
  193.9 11.7 %cholesky.286 = f32[128,128]{1,0:T(8,128)S(1)} custom-call(f32[128,128]{1,0:T(8,128)S(1)} %cholesky.426), custom_call_target="Cholesky" | custom-call | tf_op jit(solution)/shard_map/jit(cholesky)/cholesky | solution.py:43
  205.8 9.8 %custom-call.31 = f32[1,128,128]{1,2,0:T(8,128)S(1)} custom-call(f32[1,128,128]{2,1,0:T(8,128)S(1)} %get-tuple-element.87), custom_call_target="InvertDiagBlocksLowerTriangular" | custom-call | tf_op jit(solution)/shard_map/jit(cholesky)/cholesky | solution.py:43
  218.1 12.0 %cholesky.305 = f32[128,128]{1,0:T(8,128)S(1)} custom-call(f32[128,128]{1,0:T(8,128)S(1)} %cholesky.430), custom_call_target="Cholesky" | custom-call | tf_op jit(solution)/shard_map/jit(cholesky)/cholesky | solution.py:43
  230.1 9.8 %custom-call.32 = f32[1,128,128]{1,2,0:T(8,128)S(1)} custom-call(f32[1,128,128]{2,1,0:T(8,128)S(1)} %get-tuple-element.84), custom_call_target="InvertDiagBlocksLowerTriangular" | custom-call | tf_op jit(solution)/shard_map/jit(cholesky)/cholesky | solution.py:43
  241.5 11.7 %cholesky.326 = f32[128,128]{1,0:T(8,128)S(1)} custom-call(f32[128,128]{1,0:T(8,128)S(1)} %cholesky.435), custom_call_target="Cholesky" | custom-call | tf_op jit(solution)/shard_map/jit(cholesky)/cholesky | solution.py:43
  254.0 19.3 %custom-call.33 = f32[1,128,128]{1,2,0:T(8,128)S(1)} custom-call(f32[1,128,128]{2,1,0:T(8,128)S(1)} %get-tuple-element.81), custom_call_target="InvertDiagBlocksLowerTriangular" | custom-call | tf_op jit(solution)/shard_map/jit(cholesky)/cholesky | solution.py:43
  274.7 11.7 %cholesky.343 = f32[128,128]{1,0:T(8,128)S(1)} custom-call(f32[128,128]{1,0:T(8,128)S(1)} %convolution_subtract_fusion.17), custom_call_target="Cholesky" | custom-call | tf_op jit(solution)/shard_map/jit(cholesky)/cholesky | solution.py:43
  298.4 39.3 %custom-call.35 = f32[4,128,128]{1,2,0:T(8,128)S(1)} custom-call(f32[4,128,128]{2,1,0:T(8,128)S(1)} %get-tuple-element.37), custom_call_target="InvertDiagBlocksLowerTriangular" | custom-call | tf_op jit(solution)/shard_map/triangular_solve/custom-call.8 | solution.py:46
  352.0 90.2 %collective-permute-done.4 = bf16[256,8192]{1,0:T(8,128)(2,1)} collective-permute-done((bf16[256,8192]{1,0:T(8,128)(2,1)}, bf16[256,8192]{1,0:T(8,128)(2,1)}, u32[]{:S(2)}, u32[]{:S(2)}) %collective-permute-start.4) | collective-permute-done | bytes 4194336 | tf_op jit(solution)/shard_map/ppermute | solution.py:36
  447.6 10.5 %fusion.1 = f32[512,512]{0,1:T(8,128)} fusion(bf16[256,8192]{1,0:T(8,128)(2,1)} %get-tuple-element.65, bf16[256,8192]{1,0:T(8,128)(2,1)S(1)} %get-tuple-element.64), kind=kOutput, calls=%fused_computation.9 | convolution fusion | flops 4311744512 | bytes 9437184 | tf_op jit(solution)/shard_map/dot_general | solution.py:62
  464.2 23.5 %collective-permute-done.6 = f32[512,512]{0,1:T(8,128)S(1)} collective-permute-done((f32[512,512]{0,1:T(8,128)S(1)}, f32[512,512]{0,1:T(8,128)S(1)}, u32[]{:S(2)}, u32[]{:S(2)}) %collective-permute-start.6) | collective-permute-done | bytes 1048608 | tf_op jit(solution)/shard_map/ppermute | solution.py:19
  491.4 45.4 %collective-permute-done.7 = f32[512,512]{0,1:T(8,128)S(1)} collective-permute-done((f32[512,512]{0,1:T(8,128)S(1)}, f32[512,512]{0,1:T(8,128)S(1)}, u32[]{:S(2)}, u32[]{:S(2)}) %collective-permute-start.7) | collective-permute-done | bytes 1048608 | tf_op jit(solution)/shard_map/ppermute | solution.py:19
  542.2 11.7 %cholesky.358 = f32[128,128]{1,0:T(8,128)S(1)} custom-call(f32[128,128]{1,0:T(8,128)S(1)} %cholesky.439), custom_call_target="Cholesky" | custom-call | tf_op jit(solution)/shard_map/jit(cholesky)/cholesky | solution.py:43
  554.1 9.8 %custom-call.36 = f32[1,128,128]{1,2,0:T(8,128)S(1)} custom-call(f32[1,128,128]{2,1,0:T(8,128)S(1)} %get-tuple-element.77), custom_call_target="InvertDiagBlocksLowerTriangular" | custom-call | tf_op jit(solution)/shard_map/jit(cholesky)/cholesky | solution.py:43
  566.6 11.7 %cholesky.377 = f32[128,128]{1,0:T(8,128)S(1)} custom-call(f32[128,128]{1,0:T(8,128)S(1)} %cholesky.443), custom_call_target="Cholesky" | custom-call | tf_op jit(solution)/shard_map/jit(cholesky)/cholesky | solution.py:43
  579.7 9.8 %custom-call.37 = f32[1,128,128]{1,2,0:T(8,128)S(1)} custom-call(f32[1,128,128]{2,1,0:T(8,128)S(1)} %get-tuple-element.74), custom_call_target="InvertDiagBlocksLowerTriangular" | custom-call | tf_op jit(solution)/shard_map/jit(cholesky)/cholesky | solution.py:43
  591.1 11.7 %cholesky.398 = f32[128,128]{1,0:T(8,128)S(1)} custom-call(f32[128,128]{1,0:T(8,128)S(1)} %cholesky.448), custom_call_target="Cholesky" | custom-call | tf_op jit(solution)/shard_map/jit(cholesky)/cholesky | solution.py:43
  603.5 10.0 %custom-call.38 = f32[1,128,128]{1,2,0:T(8,128)S(1)} custom-call(f32[1,128,128]{2,1,0:T(8,128)S(1)} %get-tuple-element.71), custom_call_target="InvertDiagBlocksLowerTriangular" | custom-call | tf_op jit(solution)/shard_map/jit(cholesky)/cholesky | solution.py:43
  615.0 11.7 %cholesky.415 = f32[128,128]{1,0:T(8,128)S(1)} custom-call(f32[128,128]{1,0:T(8,128)S(1)} %convolution_subtract_fusion.16), custom_call_target="Cholesky" | custom-call | tf_op jit(solution)/shard_map/jit(cholesky)/cholesky | solution.py:43
  638.3 39.6 %custom-call.40 = f32[4,128,128]{1,2,0:T(8,128)S(1)} custom-call(f32[4,128,128]{2,1,0:T(8,128)S(1)} %get-tuple-element.39), custom_call_target="InvertDiagBlocksLowerTriangular" | custom-call | tf_op jit(solution)/shard_map/triangular_solve/custom-call.8 | solution.py:46
  (134 shorter events, 117.2 us)
Async XLA Ops:
  0.0 93.9 %collective-permute-start = (bf16[256,8192]{1,0:T(8,128)(2,1)}, bf16[256,8192]{1,0:T(8,128)(2,1)}, u32[]{:S(2)}, u32[]{:S(2)}) collective-permute-start(bf16[256,8192]{1,0:T(8,128)(2,1)} %bitcast.133), channel_id=1, source_target_pairs={{0,8},{8,0},{16,24},{24,16},{1,9},{9,1},{17,25},{25,17},{2,10},{10... | collective-permute-start | bytes 12582920 | tf_op jit(solution)/shard_map/ppermute | solution.py:36
  98.9 10.5 %copy-start = (bf16[256,8192]{1,0:T(8,128)(2,1)}, bf16[256,8192]{1,0:T(8,128)(2,1)S(1)}, u32[]{:S(2)}) copy-start(bf16[256,8192]{1,0:T(8,128)(2,1)S(1)} %get-tuple-element.66) | copy-start | bytes 12582916
  109.5 2.9 collective-permute-start.1
  113.8 25.4 %collective-permute-start.2 = (f32[512,512]{0,1:T(8,128)S(1)}, f32[512,512]{0,1:T(8,128)S(1)}, u32[]{:S(2)}, u32[]{:S(2)}) collective-permute-start(f32[512,512]{0,1:T(8,128)S(1)} %add.67), channel_id=1, source_target_pairs={{0,2},{1,3},{2,0},{3,1},{4,6},{5,7},{6,4},{7,5},{8,10},{9,11},{10,... | collective-permute-start | bytes 3145736 | tf_op jit(solution)/shard_map/ppermute | solution.py:19
  139.3 48.0 %collective-permute-start.3 = (f32[512,512]{0,1:T(8,128)S(1)}, f32[512,512]{0,1:T(8,128)}, u32[]{:S(2)}, u32[]{:S(2)}) collective-permute-start(f32[512,512]{0,1:T(8,128)S(1)} %add.68), channel_id=1, source_target_pairs={{0,4},{1,5},{2,6},{3,7},{4,0},{5,1},{6,2},{7,3},{8,12},{9,13},{10,... | collective-permute-start | bytes 3145736 | tf_op jit(solution)/shard_map/ppermute | solution.py:19
  192.9 1.0 copy-start.5
  337.7 4.5 copy-start.1
  350.4 91.7 %collective-permute-start.4 = (bf16[256,8192]{1,0:T(8,128)(2,1)}, bf16[256,8192]{1,0:T(8,128)(2,1)}, u32[]{:S(2)}, u32[]{:S(2)}) collective-permute-start(bf16[256,8192]{1,0:T(8,128)(2,1)} %subtract_convert_fusion.1), channel_id=1, source_target_pairs={{0,16},{16,0},{8,24},{24,8},{1,17},{17,1},{9,25},{25,9},{2,18},{18... | collective-permute-start | bytes 12582920 | tf_op jit(solution)/shard_map/ppermute | solution.py:36
  447.6 10.5 %copy-start.2 = (bf16[256,8192]{1,0:T(8,128)(2,1)}, bf16[256,8192]{1,0:T(8,128)(2,1)S(1)}, u32[]{:S(2)}) copy-start(bf16[256,8192]{1,0:T(8,128)(2,1)S(1)} %get-tuple-element.64) | copy-start | bytes 12582916
  458.1 2.9 collective-permute-start.5
  462.4 25.3 %collective-permute-start.6 = (f32[512,512]{0,1:T(8,128)S(1)}, f32[512,512]{0,1:T(8,128)S(1)}, u32[]{:S(2)}, u32[]{:S(2)}) collective-permute-start(f32[512,512]{0,1:T(8,128)S(1)} %add.71), channel_id=1, source_target_pairs={{0,2},{1,3},{2,0},{3,1},{4,6},{5,7},{6,4},{7,5},{8,10},{9,11},{10,... | collective-permute-start | bytes 3145736 | tf_op jit(solution)/shard_map/ppermute | solution.py:19
  487.9 48.9 %collective-permute-start.7 = (f32[512,512]{0,1:T(8,128)S(1)}, f32[512,512]{0,1:T(8,128)S(1)}, u32[]{:S(2)}, u32[]{:S(2)}) collective-permute-start(f32[512,512]{0,1:T(8,128)S(1)} %add.72), channel_id=1, source_target_pairs={{0,4},{1,5},{2,6},{3,7},{4,0},{5,1},{6,2},{7,3},{8,12},{9,13},{10,... | collective-permute-start | bytes 3145736 | tf_op jit(solution)/shard_map/ppermute | solution.py:19
  541.2 1.0 copy-start.4
  677.9 4.5 copy-start.3
